TPU v7x, 32 devices: a whole 2x2x4 slice. The times are simulated.
32 devices in a mesh: pix: 16 (over z, y, x), lat: 2 (over core).
Axes of the slice: x: 2, y: 2, z: 4, core: 2. Of those that a mesh axis runs over, the one named last changes fastest.
Arguments:
- latents: bfloat16 [8192, 512], P('pix'), may hold values from -6 to 6
- w_send: bfloat16 [512, 512], P(None, 'lat'), may hold values from -0.25 to 0.25
- w_recv: bfloat16 [512, 512], P(None, 'lat'), may hold values from -0.25 to 0.25
- edge_bias: float32 [512], P('lat'), may hold values from -3 to 3
- w_msg: bfloat16 [512, 512], P('lat'), may hold values from -0.25 to 0.25
- w_self: bfloat16 [512, 512], P(None, 'lat'), may hold values from -0.25 to 0.25
- w_agg: bfloat16 [512, 512], P(None, 'lat'), may hold values from -0.25 to 0.25
- node_bias: float32 [512], P('lat'), may hold values from -3 to 3
- w_node: bfloat16 [512, 512], P('lat'), may hold values from -0.25 to 0.25
- norm_gain: float32 [512], replicated, may hold values from 0.25 to 1.75
- coarse_ids: int32 [128], P('pix'), may hold values from 0 to 511
- send_list: int32 [16], P('pix'), may hold values from 0 to 3
- recv_tile: int32 [512], P('pix'), may hold values from 0 to 3
- send_tile: int32 [512], P('pix'), may hold values from 0 to 6, as said below
- edge_ends: int32 [512, 2, 128], P('pix'), may hold values from 0 to 127
- edge_mask: int32 [512, 128], P('pix'), may hold values 0 or 1
- cotangent: bfloat16 [8192, 512], P('pix'), may hold values from -6 to 6
Outputs:
- new_latents: bfloat16 [8192, 512], P('pix')
- grad_latents: float32 [8192, 512], P('pix', 'lat')
- grad_w_send: float32 [512, 512], P(None, 'lat')
- grad_w_recv: float32 [512, 512], P(None, 'lat')
- grad_edge_bias: float32 [512], P('lat')
- grad_w_msg: float32 [512, 512], P('lat')
- grad_w_self: float32 [512, 512], P(None, 'lat')
- grad_w_agg: float32 [512, 512], P(None, 'lat')
- grad_node_bias: float32 [512], P('lat')
- grad_w_node: float32 [512, 512], P('lat')
- grad_gain: float32 [512], replicated
Inputs may be any that keep to these rules, and one draw needn't show every extreme that they name: `send_tile`: a block's sender tile, numbered as in the first step: first the device's own tiles, then the 1 lent tiles of the preceding and of the following pixel range, then the 1 tiles of the coarse panel; in each device's own run of 32 blocks, the first names a tile lent by the preceding range and the second one lent by the following range. `coarse_ids`: rows may repeat.
All inputs are finite; a program needn't handle non-finite values. No bound on the sum of `edge_mask` on one device may be relied on, other than what follows from the above.
Results may differ from a plain program's by a relative error of at most 0.0085.
Values may be sent and summed in bfloat16 or wider, within the bound.
A program may use at most 128 MiB of HBM per device.

v0:
```python
import math
import jax
import jax.numpy as jnp
from jax import lax
from jax.sharding import PartitionSpec as P

norm_eps = 1e-05


def from_behind(block, axis, distance):
    devices = range(lax.axis_size(axis))
    route = [((i - distance) % len(devices), i) for i in devices]
    return lax.ppermute(block, axis, route)


def silu_slope(values):
    sigma = jax.nn.sigmoid(values)
    return sigma * (1.0 + values * (1.0 - sigma))


def tile_sums(values, offsets, weights, block_tiles, tile_count):
    block_count, tile_len = offsets.shape
    width = values.shape[-1]
    positions = jnp.arange(tile_len, dtype=jnp.int32)
    incidence = (offsets[:, :, None] == positions[None, None, :]).astype(jnp.float32) * weights[
        :, :, None
    ]
    per_block = jnp.einsum(
        "ben,beh->bnh",
        incidence,
        values.reshape(block_count, tile_len, width),
        precision=lax.Precision.HIGHEST,
    )
    tile_ids = jnp.arange(tile_count, dtype=jnp.int32)
    selector = (block_tiles[None, :] == tile_ids[:, None]).astype(jnp.float32)
    summed = jnp.einsum("tb,bnh->tnh", selector, per_block, precision=lax.Precision.HIGHEST)
    return summed.reshape(tile_count * tile_len, width)


def shards(
    latents,
    w_send,
    w_recv,
    edge_bias,
    w_msg,
    w_self,
    w_agg,
    node_bias,
    w_node,
    norm_gain,
    coarse_ids,
    send_list,
    recv_tile,
    send_tile,
    edge_ends,
    edge_mask,
    cotangent,
):
    node_dev, latent_width = latents.shape
    tile_len = edge_ends.shape[2]
    tiles_dev = node_dev // tile_len
    halo_rows = send_list.shape[0] * tile_len
    pix_count = lax.axis_size("pix")
    lat_count = lax.axis_size("lat")
    grad_scale = 1.0 / math.sqrt(node_dev * pix_count)
    hidden_part = w_send.shape[1]
    send_proj = jnp.dot(latents, w_send, preferred_element_type=jnp.float32)
    recv_proj = jnp.dot(latents, w_recv, preferred_element_type=jnp.float32)
    lent_rows = latents.reshape(tiles_dev, tile_len, latent_width)[send_list].reshape(
        halo_rows, latent_width
    )
    from_left = from_behind(lent_rows, "pix", 1)
    from_right = from_behind(lent_rows, "pix", -1)
    side_proj = jnp.dot(
        jnp.concatenate([from_left, from_right], axis=0), w_send, preferred_element_type=jnp.float32
    )
    panel_proj = jnp.dot(
        lax.all_gather(latents[coarse_ids], "pix", axis=0, tiled=True),
        w_send,
        preferred_element_type=jnp.float32,
    )
    source_proj = jnp.concatenate([send_proj, side_proj, panel_proj], axis=0)
    source_tiles = source_proj.shape[0] // tile_len
    sender_offs = edge_ends[:, 0, :]
    receiver_offs = edge_ends[:, 1, :]
    senders = (send_tile[:, None] * tile_len + sender_offs).reshape(-1)
    receivers = (recv_tile[:, None] * tile_len + receiver_offs).reshape(-1)
    mask_rows = edge_mask.astype(jnp.float32)
    edge_weight = mask_rows.reshape(-1)
    unit_rows = jnp.ones_like(mask_rows)
    edge_pre = source_proj[senders] + recv_proj[receivers] + edge_bias
    edge_act = jax.nn.silu(edge_pre).astype(jnp.bfloat16)
    message = jnp.dot(edge_act, w_msg, preferred_element_type=jnp.float32)
    agg_part = tile_sums(message, receiver_offs, mask_rows, recv_tile, tiles_dev)
    aggregate = lax.psum(agg_part, "lat")
    aggregate_bf = aggregate.astype(jnp.bfloat16)
    node_pre = (
        jnp.dot(latents, w_self, preferred_element_type=jnp.float32)
        + jnp.dot(aggregate_bf, w_agg, preferred_element_type=jnp.float32)
        + node_bias
    )
    node_act = jax.nn.silu(node_pre).astype(jnp.bfloat16)
    out_part = jnp.dot(node_act, w_node, preferred_element_type=jnp.float32)
    node_out = lax.psum(out_part, "lat")
    row_mean = jnp.mean(node_out, axis=-1, keepdims=True)
    centered = node_out - row_mean
    row_var = jnp.mean(centered * centered, axis=-1, keepdims=True)
    inv_std = lax.rsqrt(row_var + norm_eps)
    normed = centered * inv_std
    new_latents = (latents.astype(jnp.float32) + normed * norm_gain).astype(jnp.bfloat16)
    grad_out = cotangent.astype(jnp.float32)
    gain_sum = jnp.sum(grad_out * normed, axis=0)
    d_normed = grad_out * norm_gain
    out_cot = inv_std * (
        d_normed
        - jnp.mean(d_normed, axis=-1, keepdims=True)
        - normed * jnp.mean(d_normed * normed, axis=-1, keepdims=True)
    )
    out_cot_bf = out_cot.astype(jnp.bfloat16)
    node_w_grad = jnp.dot(node_act.T, out_cot_bf, preferred_element_type=jnp.float32)
    node_pre_cot = jnp.dot(out_cot_bf, w_node.T, preferred_element_type=jnp.float32) * silu_slope(
        node_pre
    )
    node_bias_sum = jnp.sum(node_pre_cot, axis=0)
    node_pre_bf = node_pre_cot.astype(jnp.bfloat16)
    self_w_grad = jnp.dot(latents.T, node_pre_bf, preferred_element_type=jnp.float32)
    agg_w_grad = jnp.dot(aggregate_bf.T, node_pre_bf, preferred_element_type=jnp.float32)
    latent_part = jnp.dot(node_pre_bf, w_self.T, preferred_element_type=jnp.float32)
    agg_cot_part = jnp.dot(node_pre_bf, w_agg.T, preferred_element_type=jnp.float32)
    agg_cot = lax.psum(agg_cot_part, "lat")
    agg_cot_bf = agg_cot.astype(jnp.bfloat16)
    msg_cot = agg_cot_bf[receivers] * edge_weight.astype(jnp.bfloat16)[:, None]
    msg_w_grad = jnp.dot(edge_act.T, msg_cot, preferred_element_type=jnp.float32)
    pre_cot = jnp.dot(msg_cot, w_msg.T, preferred_element_type=jnp.float32) * silu_slope(edge_pre)
    edge_bias_sum = jnp.sum(pre_cot, axis=0)
    src_cot = tile_sums(pre_cot, sender_offs, unit_rows, send_tile, source_tiles)
    dst_cot = tile_sums(pre_cot, receiver_offs, unit_rows, recv_tile, tiles_dev)
    own_grad = src_cot[:node_dev]
    left_back = src_cot[node_dev : node_dev + halo_rows]
    right_back = src_cot[node_dev + halo_rows : node_dev + 2 * halo_rows]
    panel_part = src_cot[node_dev + 2 * halo_rows :]
    to_left_owner = from_behind(left_back.astype(jnp.bfloat16), "pix", -1).astype(left_back.dtype)
    to_right_owner = from_behind(right_back.astype(jnp.bfloat16), "pix", 1).astype(right_back.dtype)
    returned = (to_left_owner + to_right_owner).reshape(send_list.shape[0], tile_len, hidden_part)
    own_grad = own_grad.reshape(tiles_dev, tile_len, hidden_part).at[send_list].add(returned)
    own_grad = own_grad.reshape(node_dev, hidden_part)
    coarse_grad = lax.psum_scatter(panel_part, "pix", scatter_dimension=0, tiled=True)
    own_grad = own_grad.at[coarse_ids].add(coarse_grad)
    src_cot_bf = own_grad.astype(jnp.bfloat16)
    dst_cot_bf = dst_cot.astype(jnp.bfloat16)
    send_w_grad = jnp.dot(latents.T, src_cot_bf, preferred_element_type=jnp.float32)
    recv_w_grad = jnp.dot(latents.T, dst_cot_bf, preferred_element_type=jnp.float32)
    latent_part = (
        latent_part
        + jnp.dot(src_cot_bf, w_send.T, preferred_element_type=jnp.float32)
        + jnp.dot(dst_cot_bf, w_recv.T, preferred_element_type=jnp.float32)
    )
    share_width = latent_width // lat_count
    lat_index = lax.axis_index("lat")
    lat_share = lax.psum_scatter(
        latent_part.astype(jnp.bfloat16), "lat", scatter_dimension=1, tiled=True
    ).astype(jnp.float32)
    grad_latents = lat_share + lax.dynamic_slice_in_dim(
        grad_out, lat_index * share_width, share_width, 1
    )
    summed = lax.psum(
        (
            send_w_grad,
            recv_w_grad,
            edge_bias_sum,
            msg_w_grad,
            self_w_grad,
            agg_w_grad,
            node_bias_sum,
            node_w_grad,
            gain_sum,
        ),
        "pix",
    )
    scaled = [grad_scale * entry for entry in summed]
    return (
        new_latents,
        grad_latents,
        scaled[0],
        scaled[1],
        scaled[2],
        scaled[3],
        scaled[4],
        scaled[5],
        scaled[6],
        scaled[7],
        scaled[8],
    )


def solution(mesh):
    return jax.shard_map(
        shards,
        mesh=mesh,
        in_specs=(
            P("pix", None),
            P(None, "lat"),
            P(None, "lat"),
            P("lat"),
            P("lat", None),
            P(None, "lat"),
            P(None, "lat"),
            P("lat"),
            P("lat", None),
            P(),
            P("pix"),
            P("pix"),
            P("pix"),
            P("pix"),
            P("pix", None, None),
            P("pix", None),
            P("pix", None),
        ),
        out_specs=(
            P("pix", None),
            P("pix", "lat"),
            P(None, "lat"),
            P(None, "lat"),
            P("lat"),
            P("lat", None),
            P(None, "lat"),
            P(None, "lat"),
            P("lat"),
            P("lat", None),
            P(),
        ),
        check_vma=False,
    )
```

profile of v0, /device:TPU:0, one launch (start us, length us, event | category | flops | bytes accessed | tf_op | source)
XLA Modules:
  0.0 465.5 jit_solution(5024926762899600851)
XLA Ops:
  8.9 3.0 collective-permute-start
  11.9 4.1 collective-permute-start.1
  16.6 1.7 gather_fusion
  18.3 38.1 %all-gather = bf16[128,512]{1,0:T(8,128)(2,1)S(1)} all-gather(bf16[8,512]{1,0:T(8,128)(2,1)S(1)} %gather_fusion), channel_id=2, replica_groups=mesh['pix'=16,'lat'=2] {'pix'}, dimensions={0}, use_global_device_ids=true | all-gather | bytes 139264 | tf_op jit(solution)/shard_map/all_gather | solution.py:78
  56.4 1.4 fusion.52
  57.8 1.1 fusion.53
  62.2 1.4 fusion.54
  63.6 1.2 fusion.51
  64.9 16.1 %gather_fusion.2 = f32[4096,256]{1,0:T(8,128)} fusion(f32[512,256]{1,0:T(8,128)S(1)} %fusion.54, s32[4096]{0:T(1024)S(1)} %broadcast_clamp_fusion), kind=kCustom, calls=%fused_computation.2 | custom fusion | bytes 8404992 | tf_op jit(solution)/shard_map/gather | solution.py:91
  81.3 16.6 %gather_fusion.1 = f32[4096,256]{1,0:T(8,128)} fusion(f32[896,256]{1,0:T(8,128)S(1)} %pad_maximum_fusion, s32[4096]{0:T(1024)S(1)} %broadcast_clamp_fusion.1), kind=kCustom, calls=%fused_computation.1 | custom fusion | bytes 8404992 | tf_op jit(solution)/shard_map/gather | solution.py:91
  97.9 4.9 %multiply_convert_fusion = bf16[4096,256]{1,0:T(8,128)(2,1)S(1)} fusion(f32[256]{0:T(256)S(1)} %copy-done.22, f32[4096,256]{1,0:T(8,128)} %gather_fusion.1, f32[4096,256]{1,0:T(8,128)} %gather_fusion.2), kind=kLoop, calls=%fused_computation.12 | loop fusion | flops 7340032 | bytes 10486784 | tf_op jit(solution)/shard_map/convert_element_type | solution.py:92
  102.9 1.3 fusion.55
  104.2 8.5 %fusion.11 = f32[32,128,512]{2,1,0:T(8,128)S(1)} fusion(f32[32,128,512]{2,1,0:T(8,128)S(1)} %bitcast.85, f32[32,128]{1,0:T(8,128)S(1)} %get-tuple-element.101, s32[32,128]{1,0:T(8,128)S(1)} %bitcast.94), kind=kOutput, calls=%fused_computation.21 | convolution fusion | flops 3222274048 | bytes 16809984 | tf_op jit(solution)/shard_map/ben,beh->bnh/dot_general | solution.py:28
  112.7 7.7 %fusion = f32[4,128,512]{2,0,1:T(4,128)S(1)} fusion(f32[32,128,512]{2,1,0:T(8,128)S(1)} %fusion.11, s32[32]{0:T(128)S(1)} %copy-done.20), kind=kOutput, calls=%fused_computation.5 | convolution fusion | flops 100663424 | bytes 9437312 | tf_op jit(solution)/shard_map/tb,bnh->tnh/dot_general | solution.py:36
  120.8 6.3 %all-reduce.10 = bf16[512,512]{1,0:T(8,128)(2,1)S(1)} all-reduce(f32[512,512]{1,0:T(8,128)S(1)} %bitcast.90), channel_id=1, replica_groups=mesh['pix'=16,'lat'=2] {'lat'}, use_global_device_ids=true, to_apply=%region_0.1 | all-reduce | flops 262144 | bytes 1572864 | tf_op jit(solution)/shard_map/psum | solution.py:95
  127.1 1.3 fusion.16
  129.2 2.2 fusion.45
  132.2 15.1 %all-reduce.7.cloned.1.call-done = f32[512,512]{1,0:T(8,128)} async-done(((f32[512,512]{1,0:T(8,128)}), f32[512,512]{1,0:T(8,128)}) %all-reduce.7.cloned.1.call-update) | async-done | bytes 1048592 | tf_op jit(solution)/shard_map/psum | solution.py:104
  147.3 1.5 reduce_sum.63
  148.8 1.5 multiply_reduce_fusion.2
  150.4 1.8 multiply_reduce_fusion
  152.2 1.3 multiply_convert_fusion.1
  153.8 1.2 fusion.44
  155.3 1.1 fusion.58
  156.5 1.3 fusion.56
  157.8 6.4 %all-reduce.11 = bf16[512,512]{1,0:T(8,128)(2,1)S(1)} all-reduce(f32[512,512]{1,0:T(8,128)S(1)} %fusion.57), channel_id=1, replica_groups=mesh['pix'=16,'lat'=2] {'lat'}, use_global_device_ids=true, to_apply=%region_6.7 | all-reduce | flops 262144 | bytes 1572864 | tf_op jit(solution)/shard_map/psum | solution.py:130
  164.2 17.5 %gather_fusion.3 = bf16[4096,512]{1,0:T(8,128)(2,1)} fusion(bf16[512,512]{1,0:T(8,128)(2,1)S(1)} %all-reduce.11, s32[4096]{0:T(1024)S(1)} %broadcast_clamp_fusion), kind=kCustom, calls=%fused_computation.3 | custom fusion | bytes 8404992 | tf_op jit(solution)/shard_map/gather | solution.py:132
  181.7 5.9 %fusion.50 = (f32[256]{0:T(256)S(1)}, f32[4096,256]{1,0:T(8,128)S(1)}) fusion(f32[256]{0:T(256)S(1)} %copy-done.22, f32[4096,256]{1,0:T(8,128)} %gather_fusion.1, f32[4096,256]{1,0:T(8,128)} %gather_fusion.2, bf16[256,512]{1,0:T(8,128)(2,1)S(1)} %copy-done, bf16[4096,512]{1,0:T(8,128)(2,1)} %gather_fusion.3, bf16[4096]{0:T(1024)(128)(2,1)S(1)} %get-tuple-element.100), kind=kOutput, calls=%fused_computation.107 | convolution fusion | flops 1087373056 | bytes 17049600 | tf_op jit(solution)/shard_map/dot_general | solution.py:134
  187.6 4.4 fusion.13
  192.0 2.7 fusion.14
  194.7 3.8 fusion.49
  198.8 5.5 %collective-permute-start.2 = (bf16[128,256]{1,0:T(8,128)(2,1)S(1)}, bf16[128,256]{1,0:T(8,128)(2,1)S(1)}, u32[]{:S(2)}, u32[]{:S(2)}) collective-permute-start(bf16[128,256]{1,0:T(8,128)(2,1)S(1)} %bitcast.97), channel_id=1, source_target_pairs={{2,0},{4,2},{6,4},{8,6},{10,8},{12,10},{14,12},{16,14},{18,16},{20... | collective-permute-start | bytes 196616 | tf_op jit(solution)/shard_map/ppermute | solution.py:13
  205.5 5.8 %fusion.17 = bf16[4,128,256]{2,0,1:T(4,128)(2,1)S(1)} fusion(f32[32,128,256]{2,1,0:T(8,128)} %fusion.13, s32[32]{0:T(128)S(1)} %copy-done.20), kind=kOutput, calls=%fused_computation.35 | convolution fusion | flops 50462848 | bytes 4456576 | tf_op jit(solution)/shard_map/tb,bnh->tnh/dot_general | solution.py:36
  212.0 1.1 convolution_bitcast_fusion.1
  214.1 1.9 broadcast_select_fusion
  215.9 4.1 scatter-add.12
  220.0 1.1 copy.56
  221.2 61.4 %reduce-scatter.3.cloned.1.call-done = f32[8,256]{1,0:T(8,128)} async-done(((f32[128,256]{1,0:T(8,128)}), f32[8,256]{1,0:T(8,128)}) %reduce-scatter.3.cloned.1.call-update) | async-done | bytes 8208 | tf_op jit(solution)/shard_map/reduce_scatter | solution.py:147
  283.6 1.6 convolution_add_fusion.1
  285.2 2.2 fusion.15
  287.5 2.1 convolution_bitcast_fusion
  289.5 4.5 fusion.6
  294.0 1.1 convolution_bitcast_fusion.2
  295.3 38.9 %all-reduce = (f32[256]{0:T(256)S(1)}, f32[256]{0:T(256)S(1)}, f32[512]{0:T(512)S(1)}) all-reduce(f32[256]{0:T(256)S(1)} %get-tuple-element.105, f32[256]{0:T(256)S(1)} %get-tuple-element.92, f32[512]{0:T(512)S(1)} %get-tuple-element.78), channel_id=1, replica_groups=mesh['pix'=16,'lat'=2] {'pix'}, use_global_device_ids=true, to_apply=%region_14.15 | all-reduce | flops 1024 | bytes 8192 | tf_op jit(solution)/shard_map/psum | solution.py:166
  335.9 1.8 dynamic-slice_add_fusion
  337.8 112.8 %all-reduce.9.cloned.1.call-done = (f32[512,256]{0,1:T(8,128)}, f32[512,256]{0,1:T(8,128)}, f32[256,512]{1,0:T(8,128)}, f32[512,256]{0,1:T(8,128)}, f32[512,256]{0,1:T(8,128)}, /*index=5*/f32[256,512]{1,0:T(8,128)}) async-done(((f32[512,256]{0,1:T(8,128)}, f32[512,256]{0,1:T(8,128)}, f32[256,512]{1,0:T(8,128)}, f32[512,256]{0,1:T(8,128)}, f32[512,256]{0,1:T(8,128)}, /*index=5*/f32[256,512]{1,0:T(8,128)}), ...) | async-done | bytes 3145744 | tf_op jit(solution)/shard_map/psum | solution.py:166
  450.6 1.2 broadcast_multiply_fusion.5
  452.8 1.1 broadcast_multiply_fusion.4
  (108 shorter events, 19.7 us)
Async XLA Ops:
  7.2 95.7 %copy-start = (bf16[256,512]{1,0:T(8,128)(2,1)S(1)}, bf16[256,512]{1,0:T(8,128)(2,1)}, u32[]{:S(2)}) copy-start(bf16[256,512]{1,0:T(8,128)(2,1)} %param.23) | copy-start | bytes 786436
  7.2 56.4 %copy-start.1 = (bf16[512,512]{1,0:T(8,128)(2,1)S(1)}, bf16[512,512]{1,0:T(8,128)(2,1)}, u32[]{:S(2)}) copy-start(bf16[512,512]{1,0:T(8,128)(2,1)} %param.19) | copy-start | bytes 1572868
  7.2 140.1 %all-reduce.7.cloned.1.call-start = ((), (), s32[]{:S(2)}) async-start(), calls=%async_computation.2 | async-start | bytes 2097152 | tf_op jit(solution)/shard_map/psum | solution.py:104
  8.9 72.1 %collective-permute-start = (bf16[128,512]{1,0:T(8,128)(2,1)S(1)}, bf16[128,512]{1,0:T(8,128)(2,1)S(1)}, u32[]{:S(2)}, u32[]{:S(2)}) collective-permute-start(bf16[128,512]{1,0:T(8,128)(2,1)S(1)} %dynamic-slice_bitcast_fusion), channel_id=1, source_target_pairs={{30,0},{0,2},{2,4},{4,6},{6,8},{8,10},{10,12},{12,14},{14,16},{16,... | collective-permute-start | bytes 393224 | tf_op jit(solution)/shard_map/ppermute | solution.py:13
  11.9 69.1 %collective-permute-start.1 = (bf16[128,512]{1,0:T(8,128)(2,1)S(1)}, bf16[128,512]{1,0:T(8,128)(2,1)S(1)}, u32[]{:S(2)}, u32[]{:S(2)}) collective-permute-start(bf16[128,512]{1,0:T(8,128)(2,1)S(1)} %dynamic-slice_bitcast_fusion), channel_id=1, source_target_pairs={{2,0},{4,2},{6,4},{8,6},{10,8},{12,10},{14,12},{16,14},{18,16},{20... | collective-permute-start | bytes 393224 | tf_op jit(solution)/shard_map/ppermute | solution.py:13
  64.9 16.1 %copy-start.18 = (s32[32,128]{1,0:T(8,128)S(1)}, s32[32,128]{1,0:T(8,128)}, u32[]{:S(2)}) copy-start(s32[32,128]{1,0:T(8,128)} %param.34) | copy-start | bytes 49156
  64.9 16.1 %copy-start.8 = (bf16[512,256]{1,0:T(8,128)(2,1)S(1)}, bf16[512,256]{1,0:T(8,128)(2,1)}, u32[]{:S(2)}) copy-start(bf16[512,256]{1,0:T(8,128)(2,1)} %param.20) | copy-start | bytes 786436
  81.3 16.6 %copy-start.22 = (f32[256]{0:T(256)S(1)}, f32[256]{0:T(256)}, u32[]{:S(2)}) copy-start(f32[256]{0:T(256)} %param.22) | copy-start | bytes 3076
  102.8 1.3 copy-start.3
  104.2 8.5 %copy-start.20 = (s32[32]{0:T(128)S(1)}, s32[32]{0:T(128)}, u32[]{:S(2)}) copy-start(s32[32]{0:T(128)} %param.31) | copy-start | bytes 388
  112.7 14.3 %copy-start.21 = (f32[256]{0:T(256)S(1)}, f32[256]{0:T(256)}, u32[]{:S(2)}) copy-start(f32[256]{0:T(256)} %param.26) | copy-start | bytes 3076
  120.4 11.1 %copy-start.24 = (s32[3]{0:T(128)S(1)}, s32[3]{0:T(128)}, u32[]{:S(2)}) copy-start(s32[3]{0:T(128)} %constant.62.clone.1) | copy-start | bytes 40
  127.1 23.3 %copy-start.5 = (bf16[512,512]{1,0:T(8,128)(2,1)S(1)}, bf16[512,512]{1,0:T(8,128)(2,1)}, u32[]{:S(2)}) copy-start(bf16[512,512]{1,0:T(8,128)(2,1)} %param.35) | copy-start | bytes 1572868
  127.1 23.3 %copy-start.19 = (f32[512]{0:T(512)S(1)}, f32[512]{0:T(512)}, u32[]{:S(2)}) copy-start(f32[512]{0:T(512)} %param.28) | copy-start | bytes 6148
  128.4 0.8 copy-start.12
  131.4 22.0 %copy-start.13 = (f32[512,256]{1,0:T(8,128)S(1)}, f32[512,256]{1,0:T(8,128)}, u32[]{:S(2)}) copy-start(f32[512,256]{1,0:T(8,128)} %copy-done.12) | copy-start | bytes 1572868
  131.5 151.1 %reduce-scatter.3.cloned.1.call-start = ((), (), s32[]{:S(2)}) async-start(), calls=%async_computation.3 | async-start | bytes 139264 | tf_op jit(solution)/shard_map/reduce_scatter | solution.py:147
  147.3 4.8 %copy-start.2 = (f32[512,512]{1,0:T(8,128)S(1)}, f32[512,512]{1,0:T(8,128)}, u32[]{:S(2)}) copy-start(f32[512,512]{1,0:T(8,128)} %all-reduce.7.cloned.1.call-done) | copy-start | bytes 3145732
  148.8 4.7 copy-start.25
  153.4 1.6 copy-start.10
  153.4 3.0 copy-start.11
  153.8 2.7 copy-start.7
  192.0 2.7 copy-start.23
  198.8 15.3 %collective-permute-start.2 = (bf16[128,256]{1,0:T(8,128)(2,1)S(1)}, bf16[128,256]{1,0:T(8,128)(2,1)S(1)}, u32[]{:S(2)}, u32[]{:S(2)}) collective-permute-start(bf16[128,256]{1,0:T(8,128)(2,1)S(1)} %bitcast.97), channel_id=1, source_target_pairs={{2,0},{4,2},{6,4},{8,6},{10,8},{12,10},{14,12},{16,14},{18,16},{20... | collective-permute-start | bytes 196616 | tf_op jit(solution)/shard_map/ppermute | solution.py:13
  204.3 9.7 %collective-permute-start.3 = (bf16[128,256]{1,0:T(8,128)(2,1)S(1)}, bf16[128,256]{1,0:T(8,128)(2,1)S(1)}, u32[]{:S(2)}, u32[]{:S(2)}) collective-permute-start(bf16[128,256]{1,0:T(8,128)(2,1)S(1)} %bitcast.98), channel_id=1, source_target_pairs={{30,0},{0,2},{2,4},{4,6},{6,8},{8,10},{10,12},{12,14},{14,16},{16,... | collective-permute-start | bytes 196616 | tf_op jit(solution)/shard_map/ppermute | solution.py:13
  205.2 130.8 %reduce-scatter.5.cloned.1.call-start = ((), (), s32[]{:S(2)}) async-start(), calls=%async_computation.4 | async-start | bytes 786432 | tf_op jit(solution)/shard_map/reduce_scatter | solution.py:160
  211.3 0.7 copy-start.9
  215.9 73.6 %copy-start.4 = (bf16[4096,256]{1,0:T(8,128)(2,1)S(1)}, bf16[4096,256]{1,0:T(8,128)(2,1)}, u32[]{:S(2)}) copy-start(bf16[4096,256]{1,0:T(8,128)(2,1)} %copy-done.3) | copy-start | bytes 6291460
  287.4 163.2 %all-reduce.9.cloned.1.call-start = ((), (), s32[]{:S(2)}) async-start(), calls=%async_computation.5 | async-start | bytes 6291456 | tf_op jit(solution)/shard_map/psum | solution.py:166
  294.0 1.2 copy-start.6
  450.6 4.3 copy-start.17
  450.6 5.4 %copy-start.16 = (f32[512,256]{0,1:T(8,128)S(1)}, f32[512,256]{0,1:T(8,128)}, u32[]{:S(2)}) copy-start(f32[512,256]{0,1:T(8,128)} %get-tuple-element.88) | copy-start | bytes 1572868
  450.6 6.4 %copy-start.15 = (f32[256,512]{1,0:T(8,128)S(1)}, f32[256,512]{1,0:T(8,128)}, u32[]{:S(2)}) copy-start(f32[256,512]{1,0:T(8,128)} %get-tuple-element.89) | copy-start | bytes 1572868
  451.8 6.1 %copy-start.14 = (f32[256,512]{1,0:T(8,128)S(1)}, f32[256,512]{1,0:T(8,128)}, u32[]{:S(2)}) copy-start(f32[256,512]{1,0:T(8,128)} %get-tuple-element.86) | copy-start | bytes 1572868
Sparse Core Ops, SparseCore 0:
  131.6 15.7 all-reduce.6
  205.3 77.1 reduce-scatter.2
  287.5 4.2 reduce-scatter.4
  299.8 150.6 all-reduce.8
where the time goes:
time: 469 us; the launch traced here: 465 us
  waiting for transfers between devices  189 us (40%)
  blocking collectives  89.7 us (19%)
  local copies, waits for them, and re-layouts  67 us (14%)
  matrix products  65.9 us (14%)
  other arithmetic  25.2 us (5%)
  between operations  15.3 us (3%)
  starting transfers between devices  13 us (3%)
    psum x1, waiting for transfers between devices, shards(): lax.psum((send_w_grad, recv_w_grad, edge_bias_sum, msg_w_grad, self_w_gra...  113 us
    reduce_scatter x1, waiting for transfers between devices, shards(): lax.psum_scatter(panel_part, 'pix', scatter_dimension=0, tiled=True)  61.4 us
    psum x1, blocking collectives, shards(): lax.psum((send_w_grad, recv_w_grad, edge_bias_sum, msg_w_grad, self_w_gra...  38.9 us
    all_gather x1, blocking collectives, shards(): lax.all_gather(latents[coarse_ids], 'pix', axis=0, tiled=True)  38.1 us
    gather x2, local copies, waits for them, and re-layouts, shards(): edge_pre = source_proj[senders] + recv_proj[receivers] + edge_bias  32.7 us
    gather x1, local copies, waits for them, and re-layouts, shards(): msg_cot = agg_cot_bf[receivers] * edge_weight.astype(jnp.bfloat16)[:, None]  17.5 us
    dot_general x3, matrix products, tile_sums(): jnp.einsum('tb,bnh->tnh', selector, per_block, precision=lax.Precision.HI...  17.3 us
    dot_general x3, matrix products, tile_sums(): jnp.einsum('ben,beh->bnh', incidence, values.reshape(block_count, tile_le...  15.6 us
  transfers between devices with their start and end apart: 8, of which 3 were waited for; matrix products, arithmetic and copies ran while one was open for 12% of the time, Pallas kernels for 0%

commit v1 on v0

--- a/solution.py
+++ b/solution.py
@@ -5,6 +5,18 @@
 from jax.sharding import PartitionSpec as P
 
 norm_eps = 1e-05
+
+
+def gather_by_bits(x, axis, dim):
+    ways, here = (lax.axis_size(axis), lax.axis_index(axis))
+    grown, reach = (x, 1)
+    while reach < ways:
+        theirs = lax.ppermute(grown, axis, [(d, d ^ reach) for d in range(ways)])
+        mine_first = jnp.concatenate([grown, theirs], axis=dim)
+        theirs_first = jnp.concatenate([theirs, grown], axis=dim)
+        grown = jnp.where(here & reach == 0, mine_first, theirs_first)
+        reach = 2 * reach
+    return grown
 
 
 def from_behind(block, axis, distance):
@@ -75,9 +87,7 @@
         jnp.concatenate([from_left, from_right], axis=0), w_send, preferred_element_type=jnp.float32
     )
     panel_proj = jnp.dot(
-        lax.all_gather(latents[coarse_ids], "pix", axis=0, tiled=True),
-        w_send,
-        preferred_element_type=jnp.float32,
+        gather_by_bits(latents[coarse_ids], "pix", 0), w_send, preferred_element_type=jnp.float32
     )
     source_proj = jnp.concatenate([send_proj, side_proj, panel_proj], axis=0)
     source_tiles = source_proj.shape[0] // tile_len

time: 469 us -> 439 us (0.936)
  blocking collectives: 89.7 us -> 51.4 us
  waiting for transfers between devices: 189 us -> 200 us
    all_gather x1 -> x0, blocking collectives: 38.1 us -> none  [shards(): lax.all_gather(latents[coarse_ids], 'pix', axis=0, tiled=True)]
    ppermute x0 -> x4, waiting for transfers between devices: none -> 7.59 us  [gather_by_bits(): theirs = lax.ppermute(grown, axis, [(d, d ^ reach) for d in range(ways)])]
  transfers between devices with their start and end apart: 8 -> 12, of which waited for: 3 -> 5; matrix products, arithmetic and copies ran while one was open for 12% -> 12% of each run, Pallas kernels for 0% -> 0%
where the time goes in v1:
time: 439 us; the launch traced here: 435 us
  waiting for transfers between devices  200 us (46%)
  local copies, waits for them, and re-layouts  65.3 us (15%)
  matrix products  64.3 us (15%)
  blocking collectives  51.4 us (12%)
  other arithmetic  24.4 us (6%)
  between operations  15.4 us (4%)
  starting transfers between devices  14.2 us (3%)
    psum x1, waiting for transfers between devices, shards(): lax.psum((send_w_grad, recv_w_grad, edge_bias_sum, msg_w_grad, self_w_gra...  113 us
    reduce_scatter x1, waiting for transfers between devices, shards(): lax.psum_scatter(panel_part, 'pix', scatter_dimension=0, tiled=True)  61.4 us
    psum x1, blocking collectives, shards(): lax.psum((send_w_grad, recv_w_grad, edge_bias_sum, msg_w_grad, self_w_gra...  38.7 us
    gather x2, local copies, waits for them, and re-layouts, shards(): edge_pre = source_proj[senders] + recv_proj[receivers] + edge_bias  32.6 us
    psum x1, waiting for transfers between devices, shards(): node_out = lax.psum(out_part, 'lat')  18.3 us
    gather x1, local copies, waits for them, and re-layouts, shards(): msg_cot = agg_cot_bf[receivers] * edge_weight.astype(jnp.bfloat16)[:, None]  17.5 us
    dot_general x3, matrix products, tile_sums(): jnp.einsum('tb,bnh->tnh', selector, per_block, precision=lax.Precision.HI...  17.3 us
    dot_general x3, matrix products, tile_sums(): jnp.einsum('ben,beh->bnh', incidence, values.reshape(block_count, tile_le...  15.6 us
  transfers between devices with their start and end apart: 12, of which 5 were waited for; matrix products, arithmetic and copies ran while one was open for 12% of the time, Pallas kernels for 0%

profile of v1, /device:TPU:0, one launch (start us, length us, event | category | flops | bytes accessed | tf_op | source)
XLA Modules:
  0.0 435.4 jit_solution(10392561790696740265)
XLA Ops:
  8.9 3.0 collective-permute-start
  11.9 4.1 collective-permute-start.1
  16.6 1.7 gather_fusion
  18.3 1.4 fusion.60
  21.1 1.4 fusion.61
  22.5 1.4 fusion.59
  24.3 3.7 collective-permute-done.3
  28.1 3.9 collective-permute-done.4
  32.9 16.1 %gather_fusion.2 = f32[4096,256]{1,0:T(8,128)} fusion(f32[512,256]{1,0:T(8,128)S(1)} %fusion.61, s32[4096]{0:T(1024)S(1)} %broadcast_clamp_fusion), kind=kCustom, calls=%fused_computation.2 | custom fusion | bytes 8404992 | tf_op jit(solution)/shard_map/gather | solution.py:101
  49.5 16.6 %gather_fusion.1 = f32[4096,256]{1,0:T(8,128)} fusion(f32[896,256]{1,0:T(8,128)S(1)} %pad_maximum_fusion, s32[4096]{0:T(1024)S(1)} %broadcast_clamp_fusion.1), kind=kCustom, calls=%fused_computation.1 | custom fusion | bytes 8404992 | tf_op jit(solution)/shard_map/gather | solution.py:101
  66.1 4.9 %multiply_convert_fusion = bf16[4096,256]{1,0:T(8,128)(2,1)S(1)} fusion(f32[256]{0:T(256)S(1)} %copy-done.24, f32[4096,256]{1,0:T(8,128)} %gather_fusion.1, f32[4096,256]{1,0:T(8,128)} %gather_fusion.2), kind=kLoop, calls=%fused_computation.12 | loop fusion | flops 7340032 | bytes 10486784 | tf_op jit(solution)/shard_map/convert_element_type | solution.py:102
  71.0 1.2 fusion.62
  72.4 8.5 %fusion.11 = f32[32,128,512]{2,1,0:T(8,128)S(1)} fusion(f32[32,128,512]{2,1,0:T(8,128)S(1)} %bitcast.84, f32[32,128]{1,0:T(8,128)S(1)} %get-tuple-element.101, s32[32,128]{1,0:T(8,128)S(1)} %bitcast.93), kind=kOutput, calls=%fused_computation.21 | convolution fusion | flops 3222274048 | bytes 16809984 | tf_op jit(solution)/shard_map/ben,beh->bnh/dot_general | solution.py:40
  80.9 7.7 %fusion = f32[4,128,512]{2,0,1:T(4,128)S(1)} fusion(f32[32,128,512]{2,1,0:T(8,128)S(1)} %fusion.11, s32[32]{0:T(128)S(1)} %copy-done.22), kind=kOutput, calls=%fused_computation.5 | convolution fusion | flops 100663424 | bytes 9437312 | tf_op jit(solution)/shard_map/tb,bnh->tnh/dot_general | solution.py:48
  89.0 6.3 %all-reduce.10 = bf16[512,512]{1,0:T(8,128)(2,1)S(1)} all-reduce(f32[512,512]{1,0:T(8,128)S(1)} %bitcast.89), channel_id=1, replica_groups=mesh['pix'=16,'lat'=2] {'lat'}, use_global_device_ids=true, to_apply=%region_0.1 | all-reduce | flops 262144 | bytes 1572864 | tf_op jit(solution)/shard_map/psum | solution.py:105
  95.6 2.4 fusion.53
  98.8 18.3 %all-reduce.7.cloned.1.call-done = f32[512,512]{1,0:T(8,128)} async-done(((f32[512,512]{1,0:T(8,128)}), f32[512,512]{1,0:T(8,128)}) %all-reduce.7.cloned.1.call-update) | async-done | bytes 1048592 | tf_op jit(solution)/shard_map/psum | solution.py:114
  117.1 1.5 reduce_sum.63
  118.6 1.5 multiply_reduce_fusion.2
  120.2 1.8 multiply_reduce_fusion
  122.0 1.3 multiply_convert_fusion.1
  123.6 1.2 fusion.52
  125.2 1.1 fusion.65
  126.3 1.3 fusion.63
  127.7 6.3 %all-reduce.11 = bf16[512,512]{1,0:T(8,128)(2,1)S(1)} all-reduce(f32[512,512]{1,0:T(8,128)S(1)} %fusion.64), channel_id=1, replica_groups=mesh['pix'=16,'lat'=2] {'lat'}, use_global_device_ids=true, to_apply=%region_6.7 | all-reduce | flops 262144 | bytes 1572864 | tf_op jit(solution)/shard_map/psum | solution.py:140
  134.0 17.5 %gather_fusion.3 = bf16[4096,512]{1,0:T(8,128)(2,1)} fusion(bf16[512,512]{1,0:T(8,128)(2,1)S(1)} %all-reduce.11, s32[4096]{0:T(1024)S(1)} %broadcast_clamp_fusion), kind=kCustom, calls=%fused_computation.3 | custom fusion | bytes 8404992 | tf_op jit(solution)/shard_map/gather | solution.py:142
  151.5 5.9 %fusion.58 = (f32[256]{0:T(256)S(1)}, f32[4096,256]{1,0:T(8,128)S(1)}) fusion(f32[256]{0:T(256)S(1)} %copy-done.24, f32[4096,256]{1,0:T(8,128)} %gather_fusion.1, f32[4096,256]{1,0:T(8,128)} %gather_fusion.2, bf16[256,512]{1,0:T(8,128)(2,1)S(1)} %copy-done, bf16[4096,512]{1,0:T(8,128)(2,1)} %gather_fusion.3, bf16[4096]{0:T(1024)(128)(2,1)S(1)} %get-tuple-element.100), kind=kOutput, calls=%fused_computation.119 | convolution fusion | flops 1087373056 | bytes 17049600 | tf_op jit(solution)/shard_map/dot_general | solution.py:144
  157.4 4.4 %fusion.13 = f32[32,128,256]{2,1,0:T(8,128)} fusion(f32[32,128,256]{2,1,0:T(8,128)S(1)} %bitcast.86, s32[32,128]{1,0:T(8,128)S(1)} %bitcast.94), kind=kOutput, calls=%fused_computation.24 | convolution fusion | flops 1611137024 | bytes 8404992 | tf_op jit(solution)/shard_map/ben,beh->bnh/dot_general | solution.py:40
  161.8 2.7 fusion.14
  164.5 3.8 fusion.57
  168.6 5.5 %collective-permute-start.6 = (bf16[128,256]{1,0:T(8,128)(2,1)S(1)}, bf16[128,256]{1,0:T(8,128)(2,1)S(1)}, u32[]{:S(2)}, u32[]{:S(2)}) collective-permute-start(bf16[128,256]{1,0:T(8,128)(2,1)S(1)} %bitcast.96), channel_id=1, source_target_pairs={{2,0},{4,2},{6,4},{8,6},{10,8},{12,10},{14,12},{16,14},{18,16},{20... | collective-permute-start | bytes 196616 | tf_op jit(solution)/shard_map/ppermute | solution.py:25
  175.3 5.8 %fusion.17 = bf16[4,128,256]{2,0,1:T(4,128)(2,1)S(1)} fusion(f32[32,128,256]{2,1,0:T(8,128)} %fusion.13, s32[32]{0:T(128)S(1)} %copy-done.22), kind=kOutput, calls=%fused_computation.35 | convolution fusion | flops 50462848 | bytes 4456576 | tf_op jit(solution)/shard_map/tb,bnh->tnh/dot_general | solution.py:48
  181.9 1.1 convolution_bitcast_fusion.1
  183.9 1.9 broadcast_select_fusion
  185.8 4.1 scatter-add.12
  189.9 1.1 copy.56
  191.0 61.4 %reduce-scatter.3.cloned.1.call-done = f32[8,256]{1,0:T(8,128)} async-done(((f32[128,256]{1,0:T(8,128)}), f32[8,256]{1,0:T(8,128)}) %reduce-scatter.3.cloned.1.call-update) | async-done | bytes 8208 | tf_op jit(solution)/shard_map/reduce_scatter | solution.py:157
  252.4 1.0 scatter_fusion
  253.5 1.6 convolution_add_fusion.1
  255.1 2.2 fusion.15
  257.3 2.1 convolution_bitcast_fusion
  259.4 4.5 %fusion.6 = f32[256,512]{1,0:T(8,128)} fusion(bf16[4096,256]{1,0:T(8,128)(2,1)S(1)} %copy-done.4, bf16[4096,512]{1,0:T(8,128)(2,1)} %gather_fusion.3, bf16[4096]{0:T(1024)(128)(2,1)S(1)} %get-tuple-element.100), kind=kOutput, calls=%fused_computation.15 | convolution fusion | flops 1075838976 | bytes 6823936 | tf_op jit(solution)/shard_map/dot_general | solution.py:143
  263.9 1.1 convolution_bitcast_fusion.2
  265.2 38.7 %all-reduce = (f32[256]{0:T(256)S(1)}, f32[256]{0:T(256)S(1)}, f32[512]{0:T(512)S(1)}) all-reduce(f32[256]{0:T(256)S(1)} %get-tuple-element.105, f32[256]{0:T(256)S(1)} %get-tuple-element.92, f32[512]{0:T(512)S(1)} %get-tuple-element.78), channel_id=1, replica_groups=mesh['pix'=16,'lat'=2] {'pix'}, use_global_device_ids=true, to_apply=%region_14.15 | all-reduce | flops 1024 | bytes 8192 | tf_op jit(solution)/shard_map/psum | solution.py:176
  305.6 1.8 dynamic-slice_add_fusion
  307.5 113.0 %all-reduce.9.cloned.1.call-done = (f32[512,256]{0,1:T(8,128)}, f32[512,256]{0,1:T(8,128)}, f32[256,512]{1,0:T(8,128)}, f32[512,256]{0,1:T(8,128)}, f32[512,256]{0,1:T(8,128)}, /*index=5*/f32[256,512]{1,0:T(8,128)}) async-done(((f32[512,256]{0,1:T(8,128)}, f32[512,256]{0,1:T(8,128)}, f32[256,512]{1,0:T(8,128)}, f32[512,256]{0,1:T(8,128)}, f32[512,256]{0,1:T(8,128)}, /*index=5*/f32[256,512]{1,0:T(8,128)}), ...) | async-done | bytes 3145744 | tf_op jit(solution)/shard_map/psum | solution.py:176
  420.5 1.2 broadcast_multiply_fusion.5
  422.7 1.1 broadcast_multiply_fusion.4
  (122 shorter events, 17.9 us)
Async XLA Ops:
  7.2 63.8 %copy-start = (bf16[256,512]{1,0:T(8,128)(2,1)S(1)}, bf16[256,512]{1,0:T(8,128)(2,1)}, u32[]{:S(2)}) copy-start(bf16[256,512]{1,0:T(8,128)(2,1)} %param.23) | copy-start | bytes 786436
  7.2 16.8 %copy-start.19 = (s32[32,2,128]{2,1,0:T(2,128)S(1)}, s32[32,2,128]{2,1,0:T(2,128)}, u32[]{:S(2)}) copy-start(s32[32,2,128]{2,1,0:T(2,128)} %param.33) | copy-start | bytes 98308
  7.2 25.7 %copy-start.20 = (s32[32,128]{1,0:T(8,128)S(1)}, s32[32,128]{1,0:T(8,128)}, u32[]{:S(2)}) copy-start(s32[32,128]{1,0:T(8,128)} %param.34) | copy-start | bytes 49156
  7.2 109.9 %all-reduce.7.cloned.1.call-start = ((), (), s32[]{:S(2)}) async-start(), calls=%async_computation.2 | async-start | bytes 2097152 | tf_op jit(solution)/shard_map/psum | solution.py:114
  8.9 40.3 %collective-permute-start = (bf16[128,512]{1,0:T(8,128)(2,1)S(1)}, bf16[128,512]{1,0:T(8,128)(2,1)S(1)}, u32[]{:S(2)}, u32[]{:S(2)}) collective-permute-start(bf16[128,512]{1,0:T(8,128)(2,1)S(1)} %dynamic-slice_bitcast_fusion), channel_id=1, source_target_pairs={{30,0},{0,2},{2,4},{4,6},{6,8},{8,10},{10,12},{12,14},{14,16},{16,... | collective-permute-start | bytes 393224 | tf_op jit(solution)/shard_map/ppermute | solution.py:25
  11.9 37.4 %collective-permute-start.1 = (bf16[128,512]{1,0:T(8,128)(2,1)S(1)}, bf16[128,512]{1,0:T(8,128)(2,1)S(1)}, u32[]{:S(2)}, u32[]{:S(2)}) collective-permute-start(bf16[128,512]{1,0:T(8,128)(2,1)S(1)} %dynamic-slice_bitcast_fusion), channel_id=1, source_target_pairs={{2,0},{4,2},{6,4},{8,6},{10,8},{12,10},{14,12},{16,14},{18,16},{20... | collective-permute-start | bytes 393224 | tf_op jit(solution)/shard_map/ppermute | solution.py:25
  18.3 5.9 %collective-permute-start.2 = (bf16[8,512]{1,0:T(8,128)(2,1)S(1)}, bf16[8,512]{1,0:T(8,128)(2,1)S(1)}, u32[]{:S(2)}, u32[]{:S(2)}) collective-permute-start(bf16[8,512]{1,0:T(8,128)(2,1)S(1)} %gather_fusion), channel_id=1, source_target_pairs={{0,2},{2,0},{4,6},{6,4},{8,10},{10,8},{12,14},{14,12},{16,18},{18,... | collective-permute-start | bytes 24584 | tf_op jit(solution)/shard_map/ppermute | solution.py:14
  24.2 3.8 collective-permute-start.3
  28.0 4.0 collective-permute-start.4
  32.0 17.0 %collective-permute-start.5 = (bf16[64,512]{1,0:T(8,128)(2,1)S(1)}, bf16[64,512]{1,0:T(8,128)(2,1)S(1)}, u32[]{:S(2)}, u32[]{:S(2)}) collective-permute-start(bf16[64,512]{1,0:T(8,128)(2,1)S(1)} %maximum_select_fusion.2), channel_id=1, source_target_pairs={{0,16},{2,18},{4,20},{6,22},{8,24},{10,26},{12,28},{14,30},{16,0},... | collective-permute-start | bytes 196616 | tf_op jit(solution)/shard_map/ppermute | solution.py:14
  32.9 16.1 %copy-start.8 = (bf16[512,256]{1,0:T(8,128)(2,1)S(1)}, bf16[512,256]{1,0:T(8,128)(2,1)}, u32[]{:S(2)}) copy-start(bf16[512,256]{1,0:T(8,128)(2,1)} %param.20) | copy-start | bytes 786436
  49.5 16.6 %copy-start.24 = (f32[256]{0:T(256)S(1)}, f32[256]{0:T(256)}, u32[]{:S(2)}) copy-start(f32[256]{0:T(256)} %param.22) | copy-start | bytes 3076
  71.0 1.3 copy-start.3
  72.4 8.5 %copy-start.22 = (s32[32]{0:T(128)S(1)}, s32[32]{0:T(128)}, u32[]{:S(2)}) copy-start(s32[32]{0:T(128)} %param.31) | copy-start | bytes 388
  80.9 14.4 %copy-start.10 = (bf16[512,256]{1,0:T(8,128)(2,1)S(1)}, bf16[512,256]{1,0:T(8,128)(2,1)}, u32[]{:S(2)}) copy-start(bf16[512,256]{1,0:T(8,128)(2,1)} %param.25) | copy-start | bytes 786436
  80.9 14.4 %copy-start.23 = (f32[256]{0:T(256)S(1)}, f32[256]{0:T(256)}, u32[]{:S(2)}) copy-start(f32[256]{0:T(256)} %param.26) | copy-start | bytes 3076
  88.6 9.5 %copy-start.26 = (s32[3]{0:T(128)S(1)}, s32[3]{0:T(128)}, u32[]{:S(2)}) copy-start(s32[3]{0:T(128)} %constant.75.clone.1) | copy-start | bytes 40
  95.3 24.9 %copy-start.5 = (bf16[512,512]{1,0:T(8,128)(2,1)S(1)}, bf16[512,512]{1,0:T(8,128)(2,1)}, u32[]{:S(2)}) copy-start(bf16[512,512]{1,0:T(8,128)(2,1)} %param.35) | copy-start | bytes 1572868
  95.3 24.9 %copy-start.21 = (f32[512]{0:T(512)S(1)}, f32[512]{0:T(512)}, u32[]{:S(2)}) copy-start(f32[512]{0:T(512)} %param.28) | copy-start | bytes 6148
  95.3 26.7 %copy-start.1 = (bf16[512,512]{1,0:T(8,128)(2,1)S(1)}, bf16[512,512]{1,0:T(8,128)(2,1)}, u32[]{:S(2)}) copy-start(bf16[512,512]{1,0:T(8,128)(2,1)} %param.19) | copy-start | bytes 1572868
  95.6 3.2 copy-start.13
  98.1 154.4 %reduce-scatter.3.cloned.1.call-start = ((), (), s32[]{:S(2)}) async-start(), calls=%async_computation.3 | async-start | bytes 139264 | tf_op jit(solution)/shard_map/reduce_scatter | solution.py:157
  117.1 4.9 %copy-start.2 = (f32[512,512]{1,0:T(8,128)S(1)}, f32[512,512]{1,0:T(8,128)}, u32[]{:S(2)}) copy-start(f32[512,512]{1,0:T(8,128)} %all-reduce.7.cloned.1.call-done) | copy-start | bytes 3145732
  117.1 6.2 %copy-start.14 = (f32[512,256]{1,0:T(8,128)S(1)}, f32[512,256]{1,0:T(8,128)}, u32[]{:S(2)}) copy-start(f32[512,256]{1,0:T(8,128)} %copy-done.13) | copy-start | bytes 1572868
  118.6 4.7 %copy-start.27 = (bf16[256,512]{1,0:T(8,128)(2,1)S(1)}, bf16[256,512]{1,0:T(8,128)(2,1)}, u32[]{:S(2)}) copy-start(bf16[256,512]{1,0:T(8,128)(2,1)} %param.27) | copy-start | bytes 786436
  123.3 1.6 copy-start.11
  123.3 3.1 copy-start.12
  123.6 2.7 copy-start.7
  161.8 2.7 copy-start.25
  168.6 15.3 %collective-permute-start.6 = (bf16[128,256]{1,0:T(8,128)(2,1)S(1)}, bf16[128,256]{1,0:T(8,128)(2,1)S(1)}, u32[]{:S(2)}, u32[]{:S(2)}) collective-permute-start(bf16[128,256]{1,0:T(8,128)(2,1)S(1)} %bitcast.96), channel_id=1, source_target_pairs={{2,0},{4,2},{6,4},{8,6},{10,8},{12,10},{14,12},{16,14},{18,16},{20... | collective-permute-start | bytes 196616 | tf_op jit(solution)/shard_map/ppermute | solution.py:25
  174.1 9.7 %collective-permute-start.7 = (bf16[128,256]{1,0:T(8,128)(2,1)S(1)}, bf16[128,256]{1,0:T(8,128)(2,1)S(1)}, u32[]{:S(2)}, u32[]{:S(2)}) collective-permute-start(bf16[128,256]{1,0:T(8,128)(2,1)S(1)} %bitcast.97), channel_id=1, source_target_pairs={{30,0},{0,2},{2,4},{4,6},{6,8},{8,10},{10,12},{12,14},{14,16},{16,... | collective-permute-start | bytes 196616 | tf_op jit(solution)/shard_map/ppermute | solution.py:25
  175.0 130.6 %reduce-scatter.5.cloned.1.call-start = ((), (), s32[]{:S(2)}) async-start(), calls=%async_computation.4 | async-start | bytes 786432 | tf_op jit(solution)/shard_map/reduce_scatter | solution.py:170
  181.2 0.7 copy-start.9
  185.8 73.6 %copy-start.4 = (bf16[4096,256]{1,0:T(8,128)(2,1)S(1)}, bf16[4096,256]{1,0:T(8,128)(2,1)}, u32[]{:S(2)}) copy-start(bf16[4096,256]{1,0:T(8,128)(2,1)} %copy-done.3) | copy-start | bytes 6291460
  257.3 163.2 %all-reduce.9.cloned.1.call-start = ((), (), s32[]{:S(2)}) async-start(), calls=%async_computation.5 | async-start | bytes 6291456 | tf_op jit(solution)/shard_map/psum | solution.py:176
  263.9 1.2 copy-start.6
  420.4 4.3 copy-start.18
  420.4 5.4 %copy-start.17 = (f32[512,256]{0,1:T(8,128)S(1)}, f32[512,256]{0,1:T(8,128)}, u32[]{:S(2)}) copy-start(f32[512,256]{0,1:T(8,128)} %get-tuple-element.88) | copy-start | bytes 1572868
  420.5 6.4 %copy-start.16 = (f32[256,512]{1,0:T(8,128)S(1)}, f32[256,512]{1,0:T(8,128)}, u32[]{:S(2)}) copy-start(f32[256,512]{1,0:T(8,128)} %get-tuple-element.89) | copy-start | bytes 1572868
  421.7 6.1 %copy-start.15 = (f32[256,512]{1,0:T(8,128)S(1)}, f32[256,512]{1,0:T(8,128)}, u32[]{:S(2)}) copy-start(f32[256,512]{1,0:T(8,128)} %get-tuple-element.86) | copy-start | bytes 1572868
Sparse Core Ops, SparseCore 0:
  98.2 18.8 all-reduce.6
  175.2 77.2 reduce-scatter.2
  257.4 4.2 reduce-scatter.4
  269.7 150.6 all-reduce.8
